TPU v7x, 128 devices: a whole 4x4x4 slice. The times are simulated.
128 devices in a mesh: dp: 16 (over y, z_lo, core), tensor: 8 (over z_hi, x).
Axes of the slice: x: 4, y: 4, z: 4 (z_hi: 2, z_lo: 2; z = z_hi * 2 + z_lo), core: 2. Of those that a mesh axis runs over, the one named last changes fastest.
Arguments:
- latents: bfloat16 [16, 16, 1280, 128], P(None, 'dp', 'tensor'), may hold values from -6 to 6
- kernel: bfloat16 [9, 16, 8, 12800], P(None, 'dp', 'tensor'), may hold values from -0.0546875 to 0.0546875
- out_grad: bfloat16 [16, 16, 128, 1280], P('tensor', 'dp'), may hold values from -6 to 6
Outputs:
- conv_out: bfloat16 [16, 16, 128, 1280], P('tensor', 'dp')
- in_grad: bfloat16 [16, 16, 1280, 128], P(None, 'dp', 'tensor')
- kernel_grad: float32 [9, 16, 8, 12800], P(None, 'dp', 'tensor')
All inputs are finite; a program needn't handle non-finite values.
Results may differ from a plain program's by a relative error of at most 0.001.
Values may be sent and summed in bfloat16 or wider, within the bound.
A program may use at most 256 MiB of HBM per device.

v0:
```python
import jax
import jax.numpy as jnp
from jax import lax
from jax.experimental import pallas as pl
from jax.experimental.pallas import tpu as pltpu
from jax.sharding import PartitionSpec as P

BF = jnp.bfloat16
F32 = jnp.float32
N_COPIES = 36


def dot_nt(a, b):
    return lax.dot_general(a, b, (((1,), (1,)), ((), ())), preferred_element_type=F32)


def three_shifts(row):
    wide = row.astype(F32)
    lane = lax.broadcasted_iota(jnp.int32, wide.shape, 1)
    first = jnp.where(lane == 0, 0.0, pltpu.roll(wide, 1, 1))
    last = jnp.where(lane == 127, 0.0, pltpu.roll(wide, 127, 1))
    zeros = jnp.zeros((32, 128), F32)
    return jnp.concatenate([first, wide, last, zeros], axis=0)


def body(
    g_ref, x_ref, k_ref,
    conv_ref, in_ref, kgrad_ref,
    g_pad, gt, kall, xz, xv, xt, f, xa, xb, xl, xr, p, r1, ya, yb, yl, yr, zr,
    ss, rs,
):
    t = lax.axis_index("tensor")
    d = lax.axis_index("dp")
    zh, x = t // 4, t % 4
    y, zl, c = d // 4, (d // 2) % 2, d % 2
    e = d // 2
    x_right, x_left, x_far = (x + 1) % 4, (x + 3) % 4, (x + 2) % 4
    y_right, y_left, y_far = (y + 1) % 4, (y + 3) % 4, (y + 2) % 4
    oz = 1 - zh
    e_other = y * 2 + 1 - zl

    to_z = {"tensor": oz * 4 + x}
    to_xr = {"tensor": zh * 4 + x_right}
    to_xl = {"tensor": zh * 4 + x_left}
    to_yr = {"dp": y_right * 4 + zl * 2 + c}
    to_yl = {"dp": y_left * 4 + zl * 2 + c}
    to_zl = {"dp": y * 4 + (1 - zl) * 2 + c}
    to_core = {"dp": y * 4 + zl * 2 + 1 - c}

    barrier = pltpu.get_barrier_semaphore()
    for peer in (to_z, to_xr, to_xl, to_yr, to_yl, to_zl, to_core):
        pl.semaphore_signal(barrier, inc=1, device_id=peer, device_id_type=pl.DeviceIdType.MESH)
    pl.semaphore_wait(barrier, 7)

    def copy(n, s=None):
        src, dst, peer = plan[n]() if s is None else plan[n](s)
        at = n if s is None else n + s
        return pltpu.make_async_remote_copy(
            src_ref=src,
            dst_ref=dst,
            send_sem=ss.at[at],
            recv_sem=rs.at[at],
            device_id=peer,
            device_id_type=pl.DeviceIdType.MESH,
        )

    def start(*numbers):
        for n in numbers:
            copy(n).start()

    def got(*numbers):
        for n in numbers:
            copy(n).wait_recv()

    def rows_of(z_part, x_part):
        return g_pad.at[pl.ds(1 + 2 * (z_part * 4 + x_part), 2)]

    def row_of(z_part, x_part, which):
        return g_pad.at[pl.ds(1 + 2 * (z_part * 4 + x_part) + which, 1)]

    def same(ref, peer):
        return ref, ref, peer

    def mine():
        return rows_of(zh, x)

    def pair(block):
        return kall.at[block, c]

    def pairs(y_part):
        return kall.at[pl.ds(2 * y_part, 2), c]

    def yq_of(s):
        return (y + 2 + 3 * s) % 4

    plan = {
        0: lambda: (g_ref, mine(), to_z),
        1: lambda: (g_ref, mine(), to_xr),
        2: lambda: (g_ref, mine(), to_xl),
        3: lambda: same(rows_of(oz, x), to_xr),
        4: lambda: same(rows_of(oz, x), to_xl),
        5: lambda: same(row_of(zh, x_left, 0), to_xr),
        6: lambda: same(row_of(zh, x_right, 1), to_xl),
        7: lambda: same(row_of(oz, x_left, 0), to_xr),
        8: lambda: same(row_of(oz, x_right, 1), to_xl),
        9: lambda: (x_ref.at[pl.ds(7 * oz, 9)], xz, to_z),
        10: lambda: (k_ref, kall.at[e, c, 1], to_z),
        11: lambda: same(pair(e), to_zl),
        13: lambda: same(pair(e), to_yr),
        14: lambda: same(pair(e), to_yl),
        15: lambda: same(pair(e_other), to_yr),
        16: lambda: same(pair(e_other), to_yl),
        17: lambda: same(pair(y_left * 2 + zl), to_yr),
        18: lambda: same(pair(y_right * 2 + 1 - zl), to_yl),
        19: lambda: same(pairs(y), to_core),
        20: lambda: same(pairs(y_left), to_core),
        21: lambda: same(pairs(y_right), to_core),
        22: lambda: same(pairs(y_far), to_core),
        23: lambda: (f.at[x_far, 0], xa, to_xr),
        24: lambda: (f.at[x_far, 1], xb, to_xl),
        25: lambda: (f.at[x_right], xl, to_xr),
        26: lambda: (f.at[x_left], xr, to_xl),
        27: lambda s: (
            p.at[pl.ds(2 * yq_of(s), 2), 1 - c],
            r1.at[pl.ds(2 * yq_of(s), 2)],
            to_core,
        ),
        31: lambda: (r1.at[2 * y_far], ya, to_yr),
        32: lambda: (r1.at[2 * y_far + 1], yb, to_yl),
        33: lambda: (r1.at[pl.ds(2 * y_right, 2)], yl, to_yr),
        34: lambda: (r1.at[pl.ds(2 * y_left, 2)], yr, to_yl),
        35: lambda: (r1.at[2 * y + 1 - zl], zr, to_zl),
    }

    start(10, 0, 1, 2, 9)

    kall[e, c, 0] = k_ref[...]
    g_pad[pl.ds(1 + 2 * t, 2)] = g_ref[...]
    g_pad[0] = jnp.zeros((128, 1280), BF)
    g_pad[17] = jnp.zeros((128, 1280), BF)

    def turn(z_part, x_part):
        at = z_part * 4 + x_part
        block = g_pad[pl.ds(1 + 2 * at, 2)].reshape(256, 1280)
        gt[:, :, pl.ds(pl.multiple_of(at * 256, 256), 256)] = block.T.reshape(16, 80, 256)

    got(10)
    start(11)
    start(13)
    start(14)

    xv[:, 0:128] = jnp.zeros((512, 128), BF)
    xv[:, 17 * 128 : 18 * 128] = jnp.zeros((512, 128), BF)

    def own_row(k, _):
        at = pl.multiple_of((k + 1) * 128, 128)
        xv[:, pl.ds(at, 128)] = three_shifts(x_ref[k]).astype(BF)
        return 0

    lax.fori_loop(0, 16, own_row, 0)

    got(11)
    start(15)
    start(16)
    start(19)

    xt[0, 9 * zh] = jnp.zeros((128, 512), BF)
    xt[1, 9 * zh] = jnp.zeros((128, 512), BF)

    def own_turned(k, _):
        xt[0, k + 1 - zh] = three_shifts(x_ref[7 * zh + k]).T.astype(BF)
        return 0

    lax.fori_loop(0, 9, own_turned, 0)

    turn(zh, x)
    got(0)
    start(3)
    start(4)
    turn(oz, x)
    got(1, 2)
    start(5)
    start(6)

    got(13, 16)
    start(17)
    start(18)
    got(15)
    start(20)
    got(14)
    start(21)

    turn(zh, x_left)
    turn(zh, x_right)
    got(9)

    def other_turned(k, _):
        xt[1, k + 1 - zh] = three_shifts(xz[k]).T.astype(BF)
        return 0

    lax.fori_loop(0, 9, other_turned, 0)

    got(3, 4)
    start(7)
    start(8)
    got(17, 18)
    start(22)
    turn(oz, x_left)
    turn(oz, x_right)
    got(19, 20, 21, 22)

    def forward(s, _):
        xq = (x + 2 + 3 * s) % 4
        left = jnp.concatenate(
            [xt[j, pl.ds(2 * xq + u, 2)].reshape(256, 512) for j in range(2) for u in range(3)],
            axis=1,
        )
        right = jnp.concatenate(
            [kall[:, :, j, u].reshape(1280, 512) for j in range(2) for u in range(3)], axis=1
        )
        f[xq] = dot_nt(left, right).reshape(2, 128, 1280)

        @pl.when(s == 0)
        def _():
            start(23)
            start(24)

        return 0

    lax.fori_loop(0, 4, forward, 0)

    got(5, 6, 7, 8)
    turn(zh, x_far)
    turn(oz, x_far)

    def kernel_terms(s, _):
        yq = yq_of(s)
        left = gt[pl.ds(4 * yq, 4)].reshape(320, 2048)
        for u in range(3):
            part = dot_nt(left, xv[:, u * 128 : u * 128 + 2048])
            p[pl.ds(2 * yq, 2), :, u] = part.reshape(2, 2, 80, 512)
        copy(27, s).start()

        @pl.when(s == 1)
        def _():
            got(23)
            f[x_right, 0] = f[x_right, 0] + xa[...]
            start(25)
            got(24)
            f[x_left, 1] = f[x_left, 1] + xb[...]
            start(26)

        @pl.when(s == 2)
        def _():
            joined(0)
            start(31)
            start(32)

        return 0

    def joined(s):
        yq = yq_of(s)
        copy(27, s).wait_recv()
        for k in range(2):
            r1[2 * yq + k] = r1[2 * yq + k] + p[2 * yq + k, c]

    lax.fori_loop(0, 4, kernel_terms, 0)

    lane = lax.broadcasted_iota(jnp.int32, (160, 128), 1)

    def input_grad(s, _):
        left = jnp.concatenate(
            [g_pad[pl.ds(4 * s + 2 - u, 4)].reshape(512, 1280) for u in range(3)], axis=1
        )
        right = jnp.concatenate([kall[:, :, 0, u].reshape(1280, 512) for u in range(3)], axis=0)
        turned = jnp.dot(left, right, preferred_element_type=F32).T
        for k in range(4):
            at = slice(k * 128, (k + 1) * 128)
            first = jnp.where(lane == 127, 0.0, pltpu.roll(turned[0:160, at], 127, 1))
            last = jnp.where(lane == 0, 0.0, pltpu.roll(turned[320:480, at], 1, 1))
            in_ref[4 * s + k] = (first + turned[160:320, at] + last).astype(BF)

        @pl.when(s == 0)
        def _():
            joined(1)
            joined(3)

        @pl.when(s == 1)
        def _():
            got(31)
            r1[2 * y_right] = r1[2 * y_right] + ya[...]
            start(33)
            got(32)
            r1[2 * y_left + 1] = r1[2 * y_left + 1] + yb[...]
            start(34)

        return 0

    lax.fori_loop(0, 4, input_grad, 0)

    joined(2)
    got(25, 26)
    for k in range(2):
        conv_ref[k] = (f[x, k] + xl[k] + xr[k]).astype(BF)
    got(33, 34)
    for k in range(2):
        r1[2 * y + k] = r1[2 * y + k] + yl[k] + yr[k]
    start(35)
    got(35)
    kgrad_ref[...] = r1[2 * y + zl] + zr[...]

    for n in plan:
        if n != 27:
            copy(n).wait_send()
    for s in range(4):
        copy(27, s).wait_send()


def on_device(latents, kernel, out_grad):
    g = out_grad.reshape(2, 128, 1280)
    xs = latents.reshape(16, 160, 128)
    k = kernel.reshape(3, 3, 80, 160).transpose(0, 2, 1, 3).reshape(3, 80, 480)
    k = jnp.pad(k, ((0, 0), (0, 0), (0, 32)))
    vmem = pl.BlockSpec(memory_space=pltpu.VMEM)
    scratch = [
        ((18, 128, 1280), BF),
        ((16, 80, 2048), BF),
        ((8, 2, 2, 3, 80, 512), BF),
        ((9, 160, 128), BF),
        ((512, 2304), BF),
        ((2, 10, 128, 512), BF),
        ((4, 2, 128, 1280), F32),
        ((128, 1280), F32),
        ((128, 1280), F32),
        ((2, 128, 1280), F32),
        ((2, 128, 1280), F32),
        ((8, 2, 3, 80, 512), F32),
        ((8, 3, 80, 512), F32),
        ((3, 80, 512), F32),
        ((3, 80, 512), F32),
        ((2, 3, 80, 512), F32),
        ((2, 3, 80, 512), F32),
        ((3, 80, 512), F32),
    ]
    conv, grad, kgrad = pl.pallas_call(
        body,
        out_shape=(
            jax.ShapeDtypeStruct((2, 128, 1280), BF),
            jax.ShapeDtypeStruct((16, 160, 128), BF),
            jax.ShapeDtypeStruct((3, 80, 512), F32),
        ),
        in_specs=[vmem] * 3,
        out_specs=(vmem, vmem, vmem),
        scratch_shapes=[pltpu.VMEM(shape, dtype) for shape, dtype in scratch]
        + [pltpu.SemaphoreType.DMA((N_COPIES,)), pltpu.SemaphoreType.DMA((N_COPIES,))],
        compiler_params=pltpu.CompilerParams(
            collective_id=0, has_side_effects=True, vmem_limit_bytes=67043328
        ),
        name="conv_all",
    )(g, xs, k)
    kgrad = kgrad[:, :, :480].reshape(3, 80, 3, 160).transpose(0, 2, 1, 3)
    return (
        conv.reshape(2, 1, 128, 1280),
        grad.reshape(16, 1, 160, 128),
        kgrad.reshape(9, 1, 1, 12800),
    )


def solution(mesh):
    return jax.shard_map(
        on_device,
        mesh=mesh,
        in_specs=(
            P(None, "dp", "tensor", None),
            P(None, "dp", "tensor", None),
            P("tensor", "dp", None, None),
        ),
        out_specs=(
            P("tensor", "dp", None, None),
            P(None, "dp", "tensor", None),
            P(None, "dp", "tensor", None),
        ),
        check_vma=False,
    )
```

profile of v0, /device:TPU:0, one launch (start us, length us, event | category | flops | bytes accessed | tf_op | source)
XLA Modules:
  0.0 149.8 jit_solution(13245787366581230296)
XLA Ops:
  0.6 1.5 reshape.32
  2.1 0.3 copy.15
  2.4 0.2 copy.16
  2.5 0.7 pad.4.k_ref
  3.3 141.1 %conv_all.1 = (bf16[2,128,1280]{2,1,0:T(8,128)(2,1)}, bf16[16,160,128]{2,1,0:T(8,128)(2,1)}, f32[3,80,512]{2,1,0:T(8,128)}) custom-call(bf16[2,128,1280]{2,1,0:T(8,128)(2,1)} %bitcast.21, bf16[16,160,128]{2,1,0:T(8,128)(2,1)} %bitcast.22, bf16[3,80,512]{2,1,0:T(8,128)(2,1)} %pad.4.k_ref), custom_call_target="tpu_custom_call" | custom-call | tf_op jit(solution)/shard_map/conv_all/pallas_call | solution.py:345
  144.4 1.3 copy.17
  145.6 0.4 copy.18
  146.0 0.0 copy-start.1
  146.0 1.6 %reshape.38 = f32[9,1,1,12800]{3,2,1,0:T(1,128)} reshape(f32[3,3,80,160]{3,2,1,0:T(8,128)S(1)} %copy.18) | data formatting | bytes 921600 | tf_op jit(solution)/shard_map/reshape | solution.py:365
  147.7 0.0 copy-done.1
  147.7 0.0 copy-start
  147.7 0.8 copy.24
  148.5 0.5 copy-done
  149.0 0.8 copy.25
Async XLA Ops:
  146.0 1.6 %copy-start.1 = (bf16[2,128,1280]{2,1,0:T(8,128)(2,1)S(1)}, bf16[2,128,1280]{2,1,0:T(8,128)(2,1)}, u32[]{:S(2)}) copy-start(bf16[2,128,1280]{2,1,0:T(8,128)(2,1)} %get-tuple-element.6) | copy-start | bytes 1966084
  147.7 1.3 copy-start
where the time goes:
time: 150 us
  Pallas kernels  141 us (94%)
  local copies, waits for them, and re-layouts  8.06 us (5%)
    pallas_call x1, Pallas kernels, on_device(): pl.pallas_call(body, out_shape=(jax.ShapeDtypeStruct((2, 128, 1280), BF),...  141 us

commit v1 on v0

v1 whole, which is shorter than its diff:
```python
import jax
import jax.numpy as jnp
from jax import lax
from jax.experimental import pallas as pl
from jax.experimental.pallas import tpu as pltpu
from jax.sharding import PartitionSpec as P

BF = jnp.bfloat16
F32 = jnp.float32
N_COPIES = 49


def dot_nt(a, b):
    return lax.dot_general(a, b, (((1,), (1,)), ((), ())), preferred_element_type=F32)


def three_shifts(row):
    wide = row.astype(F32)
    lane = lax.broadcasted_iota(jnp.int32, wide.shape, 1)
    first = jnp.where(lane == 0, 0.0, pltpu.roll(wide, 1, 1))
    last = jnp.where(lane == 127, 0.0, pltpu.roll(wide, 127, 1))
    zeros = jnp.zeros((32, 128), F32)
    return jnp.concatenate([first, wide, last, zeros], axis=0)


def body(
    g_ref, x_ref, k_ref,
    conv_ref, in_ref, kgrad_ref,
    g_pad, gt, kall, xz, xv, xt, f, xa, xb, xl, xr, p, r1, ya, yb, yl, yr, zr,
    ss, rs, sc,
):
    t = lax.axis_index("tensor")
    d = lax.axis_index("dp")
    zh, x = t // 4, t % 4
    y, zl, c = d // 4, (d // 2) % 2, d % 2
    e = d // 2
    x_right, x_left, x_far = (x + 1) % 4, (x + 3) % 4, (x + 2) % 4
    y_right, y_left, y_far = (y + 1) % 4, (y + 3) % 4, (y + 2) % 4
    oz = 1 - zh
    e_other = y * 2 + 1 - zl

    to_z = {"tensor": oz * 4 + x}
    to_xr = {"tensor": zh * 4 + x_right}
    to_xl = {"tensor": zh * 4 + x_left}
    to_yr = {"dp": y_right * 4 + zl * 2 + c}
    to_yl = {"dp": y_left * 4 + zl * 2 + c}
    to_zl = {"dp": y * 4 + (1 - zl) * 2 + c}
    to_core = {"dp": y * 4 + zl * 2 + 1 - c}
    to_zx = {"tensor": oz * 4 + x, "dp": y * 4 + (1 - zl) * 2 + c}

    barrier = pltpu.get_barrier_semaphore()
    for peer in (to_z, to_xr, to_xl, to_yr, to_yl, to_zl, to_zx, to_core):
        pl.semaphore_signal(barrier, inc=1, device_id=peer, device_id_type=pl.DeviceIdType.MESH)
    pl.semaphore_wait(barrier, 8)

    def copy(n):
        src, dst, peer = plan[n]()
        return pltpu.make_async_remote_copy(
            src_ref=src,
            dst_ref=dst,
            send_sem=ss.at[n],
            recv_sem=rs.at[n],
            device_id=peer,
            device_id_type=pl.DeviceIdType.MESH,
        )

    def start(*numbers):
        for n in numbers:
            copy(n).start()

    def got(*numbers):
        for n in numbers:
            copy(n).wait_recv()

    def row_of(z_part, x_part, which):
        return g_pad.at[1 + 2 * (z_part * 4 + x_part) + which]

    def same(ref, peer):
        return ref, ref, peer

    def pair(block):
        return kall.at[block, c]

    def pairs(y_part):
        return kall.at[pl.ds(2 * y_part, 2), c]

    def part_of(s):
        return (y + 2 + 3 * s) % 4

    def half(ref, which):
        return ref.at[:, which * 40 : which * 40 + 40]

    def first_hop(k, which):
        block = 1 - zl if k == 0 else zl
        return half(r1.at[2 * y_far + block], which), (ya, yb)[which].at[k], (to_yr, to_yl)[which]

    def second_hop(k, way, which):
        block = 1 - zl if k == 0 else zl
        y_part = (y_right, y_left)[way]
        return (
            half(r1.at[2 * y_part + block], which),
            half((yl, yr)[way].at[k], which),
            (to_yr, to_yl)[way],
        )

    plan = {
        0: lambda: (g_ref.at[0], row_of(zh, x, 0), to_z),
        1: lambda: (g_ref.at[1], row_of(zh, x, 1), to_z),
        2: lambda: (k_ref, kall.at[e, c, 1], to_z),
        3: lambda: (k_ref, kall.at[e, c, 0], to_zl),
        4: lambda: (k_ref, kall.at[e, c, 1], to_zx),
        5: lambda: (x_ref.at[pl.ds(7 * oz, 9)], xz, to_z),
        6: lambda: (g_ref.at[0], row_of(zh, x, 0), to_xr),
        7: lambda: (g_ref.at[1], row_of(zh, x, 1), to_xr),
        8: lambda: (g_ref.at[1], row_of(zh, x, 1), to_xl),
        9: lambda: (g_ref.at[0], row_of(zh, x, 0), to_xl),
        10: lambda: same(row_of(zh, x_left, 0), to_xr),
        11: lambda: same(row_of(zh, x_right, 1), to_xl),
        12: lambda: same(row_of(oz, x, 0), to_xr),
        13: lambda: same(row_of(oz, x, 1), to_xr),
        14: lambda: same(row_of(oz, x, 0), to_xl),
        15: lambda: same(row_of(oz, x, 1), to_xl),
        16: lambda: same(row_of(oz, x_left, 0), to_xr),
        17: lambda: same(row_of(oz, x_right, 1), to_xl),
        18: lambda: (k_ref, kall.at[e, c, 0], to_yr),
        19: lambda: (k_ref, kall.at[e, c, 0], to_yl),
        20: lambda: same(kall.at[e, c, 1], to_yr),
        21: lambda: same(kall.at[e, c, 1], to_yl),
        22: lambda: same(pair(e_other), to_yr),
        23: lambda: same(pair(e_other), to_yl),
        24: lambda: same(pair(y_left * 2 + zl), to_yr),
        25: lambda: same(pair(y_right * 2 + 1 - zl), to_yl),
        26: lambda: same(pairs(y), to_core),
        27: lambda: same(pairs(y_left), to_core),
        28: lambda: same(pairs(y_right), to_core),
        29: lambda: same(pairs(y_far), to_core),
        30: lambda: (f.at[x_far, 0], xa, to_xr),
        31: lambda: (f.at[x_far, 1], xb, to_xl),
        32: lambda: (f.at[x_right, 1], xl.at[1], to_xr),
        33: lambda: (f.at[x_left, 0], xr.at[0], to_xl),
        34: lambda: (f.at[x_right, 0], xl.at[0], to_xr),
        35: lambda: (f.at[x_left, 1], xr.at[1], to_xl),
        36: lambda: first_hop(0, 0),
        37: lambda: first_hop(0, 1),
        38: lambda: first_hop(1, 0),
        39: lambda: first_hop(1, 1),
        40: lambda: second_hop(0, 0, 1),
        41: lambda: second_hop(0, 1, 0),
        42: lambda: second_hop(0, 0, 0),
        43: lambda: second_hop(0, 1, 1),
        44: lambda: second_hop(1, 0, 1),
        45: lambda: second_hop(1, 1, 0),
        46: lambda: second_hop(1, 0, 0),
        47: lambda: second_hop(1, 1, 1),
        48: lambda: (r1.at[2 * y + 1 - zl], zr, to_zl),
    }

    def siblings(s):
        return pltpu.make_async_remote_copy(
            src_ref=p.at[pl.ds(2 * part_of(s), 2), 1 - c],
            dst_ref=r1.at[pl.ds(2 * part_of(s), 2)],
            send_sem=sc.at[0, s],
            recv_sem=sc.at[1, s],
            device_id=to_core,
            device_id_type=pl.DeviceIdType.MESH,
        )

    start(2, 6, 8, 18, 19, 3, 4, 7, 9, 0, 1, 5)

    kall[e, c, 0] = k_ref[...]
    g_pad[pl.ds(1 + 2 * t, 2)] = g_ref[...]
    g_pad[0] = jnp.zeros((128, 1280), BF)
    g_pad[17] = jnp.zeros((128, 1280), BF)

    def turn(z_part, x_part):
        at = z_part * 4 + x_part
        block = g_pad[pl.ds(1 + 2 * at, 2)].reshape(256, 1280)
        gt[:, :, pl.ds(pl.multiple_of(at * 256, 256), 256)] = block.T.reshape(16, 80, 256)

    xv[:, 0:128] = jnp.zeros((512, 128), BF)
    xv[:, 17 * 128 : 18 * 128] = jnp.zeros((512, 128), BF)

    def own_row(k, _):
        at = pl.multiple_of((k + 1) * 128, 128)
        xv[:, pl.ds(at, 128)] = three_shifts(x_ref[k]).astype(BF)
        return 0

    lax.fori_loop(0, 16, own_row, 0)

    got(6)
    start(10)
    got(8)
    start(11)

    xt[0, 9 * zh] = jnp.zeros((128, 512), BF)
    xt[1, 9 * zh] = jnp.zeros((128, 512), BF)

    def own_turned(k, _):
        xt[0, k + 1 - zh] = three_shifts(x_ref[7 * zh + k]).T.astype(BF)
        return 0

    lax.fori_loop(0, 9, own_turned, 0)

    got(2)
    start(20, 21)
    got(3, 4)
    start(22, 23, 26)
    turn(zh, x)
    got(18, 20)
    start(24)
    got(0)
    start(12, 14)
    got(7, 9)
    turn(zh, x_left)
    turn(zh, x_right)
    got(1)
    start(13, 15)
    turn(oz, x)
    got(23)
    start(25)
    got(22)
    start(27)
    got(19, 21)
    start(28)
    got(12)
    start(16)
    got(5)

    def other_turned(k, _):
        xt[1, k + 1 - zh] = three_shifts(xz[k]).T.astype(BF)
        return 0

    lax.fori_loop(0, 9, other_turned, 0)

    got(15)
    start(17)
    got(13, 14)
    turn(oz, x_left)
    turn(oz, x_right)
    got(10, 11)
    turn(zh, x_far)
    got(24, 25)
    start(29)
    got(26, 27, 28, 29)

    def forward(xq):
        left = jnp.concatenate(
            [xt[j, pl.ds(2 * xq + u, 2)].reshape(256, 512) for j in range(2) for u in range(3)],
            axis=1,
        )
        right = jnp.concatenate(
            [kall[:, :, j, u].reshape(1280, 512) for j in range(2) for u in range(3)], axis=1
        )
        f[xq] = dot_nt(left, right).reshape(2, 128, 1280)

    def kernel_terms(s, _):
        yq = part_of(s)
        left = gt[pl.ds(4 * yq, 4)].reshape(320, 2048)
        for u in range(3):
            part = dot_nt(left, xv[:, u * 128 : u * 128 + 2048])
            p[pl.ds(2 * yq, 2), :, u] = part.reshape(2, 2, 80, 512)
        siblings(s).start()
        return 0

    def joined(s):
        siblings(s).wait_recv()
        for k in range(2):
            at = 2 * part_of(s) + k
            r1[at] = r1[at] + p[at, c]

    def add_half(k, way):
        block = 1 - zl if k == 0 else zl
        at = 2 * (y_right, y_left)[way] + block
        rows = slice(way * 40, way * 40 + 40)
        r1[at, :, rows] = r1[at, :, rows] + (ya, yb)[way][k]

    forward(x_far)
    start(30, 31)
    got(16, 17)
    turn(oz, x_far)
    lax.fori_loop(0, 2, kernel_terms, 0)
    joined(0)
    start(36, 37, 38, 39)

    def near(s, _):
        forward((x + 1 + 2 * s) % 4)

        @pl.when(s == 0)
        def _():
            start(32)

        return 0

    lax.fori_loop(0, 2, near, 0)
    start(33)
    got(30)
    f[x_right, 0] = f[x_right, 0] + xa[...]
    start(34)
    got(31)
    f[x_left, 1] = f[x_left, 1] + xb[...]
    start(35)

    def last_terms(s, _):
        kernel_terms(5 - s, 0)

        @pl.when(s == 2)
        def _():
            joined(1)
            start(40)

        return 0

    lax.fori_loop(2, 4, last_terms, 0)
    joined(3)
    start(41)
    got(36)
    add_half(0, 0)
    start(42)
    got(37)
    add_half(0, 1)
    start(43, 44, 45)
    got(38)
    add_half(1, 0)
    start(46)
    got(39)
    add_half(1, 1)
    start(47)
    joined(2)
    forward(x)

    lane = lax.broadcasted_iota(jnp.int32, (160, 128), 1)

    def input_grad(s, _):
        left = jnp.concatenate(
            [g_pad[pl.ds(4 * s + 2 - u, 4)].reshape(512, 1280) for u in range(3)], axis=1
        )
        right = jnp.concatenate([kall[:, :, 0, u].reshape(1280, 512) for u in range(3)], axis=0)
        turned = jnp.dot(left, right, preferred_element_type=F32).T
        for k in range(4):
            at = slice(k * 128, (k + 1) * 128)
            first = jnp.where(lane == 127, 0.0, pltpu.roll(turned[0:160, at], 127, 1))
            last = jnp.where(lane == 0, 0.0, pltpu.roll(turned[320:480, at], 1, 1))
            in_ref[4 * s + k] = (first + turned[160:320, at] + last).astype(BF)

        @pl.when(s == 2)
        def _():
            got(40, 41, 42, 43)
            at = 2 * y + 1 - zl
            r1[at] = r1[at] + yl[0] + yr[0]
            start(48)

        return 0

    lax.fori_loop(0, 4, input_grad, 0)

    for k, numbers in ((1, (32, 35)), (0, (33, 34))):
        got(*numbers)
        conv_ref[k] = (f[x, k] + xl[k] + xr[k]).astype(BF)
    got(44, 45, 46, 47)
    r1[2 * y + zl] = r1[2 * y + zl] + yl[1] + yr[1]
    got(48)
    kgrad_ref[...] = r1[2 * y + zl] + zr[...]

    for n in plan:
        copy(n).wait_send()
    for s in range(4):
        siblings(s).wait_send()


def on_device(latents, kernel, out_grad):
    g = out_grad.reshape(2, 128, 1280)
    xs = latents.reshape(16, 160, 128)
    k = kernel.reshape(3, 3, 80, 160).transpose(0, 2, 1, 3).reshape(3, 80, 480)
    k = jnp.pad(k, ((0, 0), (0, 0), (0, 32)))
    vmem = pl.BlockSpec(memory_space=pltpu.VMEM)
    scratch = [
        ((18, 128, 1280), BF),
        ((16, 80, 2048), BF),
        ((8, 2, 2, 3, 80, 512), BF),
        ((9, 160, 128), BF),
        ((512, 2304), BF),
        ((2, 10, 128, 512), BF),
        ((4, 2, 128, 1280), F32),
        ((128, 1280), F32),
        ((128, 1280), F32),
        ((2, 128, 1280), F32),
        ((2, 128, 1280), F32),
        ((8, 2, 3, 80, 512), F32),
        ((8, 3, 80, 512), F32),
        ((2, 3, 40, 512), F32),
        ((2, 3, 40, 512), F32),
        ((2, 3, 80, 512), F32),
        ((2, 3, 80, 512), F32),
        ((3, 80, 512), F32),
    ]
    conv, grad, kgrad = pl.pallas_call(
        body,
        out_shape=(
            jax.ShapeDtypeStruct((2, 128, 1280), BF),
            jax.ShapeDtypeStruct((16, 160, 128), BF),
            jax.ShapeDtypeStruct((3, 80, 512), F32),
        ),
        in_specs=[vmem] * 3,
        out_specs=(vmem, vmem, vmem),
        scratch_shapes=[pltpu.VMEM(shape, dtype) for shape, dtype in scratch]
        + [pltpu.SemaphoreType.DMA(shape) for shape in ((N_COPIES,), (N_COPIES,), (2, 4))],
        compiler_params=pltpu.CompilerParams(
            collective_id=0, has_side_effects=True, vmem_limit_bytes=67043328
        ),
        name="conv_all",
    )(g, xs, k)
    kgrad = kgrad[:, :, :480].reshape(3, 80, 3, 160).transpose(0, 2, 1, 3)
    return (
        conv.reshape(2, 1, 128, 1280),
        grad.reshape(16, 1, 160, 128),
        kgrad.reshape(9, 1, 1, 12800),
    )


def solution(mesh):
    return jax.shard_map(
        on_device,
        mesh=mesh,
        in_specs=(
            P(None, "dp", "tensor", None),
            P(None, "dp", "tensor", None),
            P("tensor", "dp", None, None),
        ),
        out_specs=(
            P("tensor", "dp", None, None),
            P(None, "dp", "tensor", None),
            P(None, "dp", "tensor", None),
        ),
        check_vma=False,
    )
```

time: 150 us -> 108 us (0.72)
  Pallas kernels: 141 us -> 98.8 us
    pallas_call x1, Pallas kernels: 141 us -> 98.8 us  [on_device(): pl.pallas_call(body, out_shape=(jax.ShapeDtypeStruct((2, 128, 1280), BF),...]
where the time goes in v1:
time: 108 us
  Pallas kernels  98.8 us (91%)
  local copies, waits for them, and re-layouts  8.06 us (7%)
    pallas_call x1, Pallas kernels, on_device(): pl.pallas_call(body, out_shape=(jax.ShapeDtypeStruct((2, 128, 1280), BF),...  98.8 us
    unnamed x6, local copies, waits for them, and re-layouts  2.16 us

profile of v1, /device:TPU:0, one launch (start us, length us, event | category | flops | bytes accessed | tf_op | source)
XLA Modules:
  0.0 107.6 jit_solution(1418724743737500731)
XLA Ops:
  0.6 1.5 %reshape.32 = bf16[3,3,80,160]{3,2,1,0:T(8,128)(2,1)S(1)} reshape(bf16[9,1,1,12800]{3,0,2,1:T(8,128)(2,1)} %param.4) | data formatting | bytes 460800 | tf_op jit(solution)/shard_map/reshape | solution.py:373
  2.1 0.3 copy.15
  2.4 0.2 copy.16
  2.5 0.7 pad.4.k_ref
  3.3 98.8 %conv_all.1 = (bf16[2,128,1280]{2,1,0:T(8,128)(2,1)}, bf16[16,160,128]{2,1,0:T(8,128)(2,1)}, f32[3,80,512]{2,1,0:T(8,128)}) custom-call(bf16[2,128,1280]{2,1,0:T(8,128)(2,1)} %bitcast.21, bf16[16,160,128]{2,1,0:T(8,128)(2,1)} %bitcast.22, bf16[3,80,512]{2,1,0:T(8,128)(2,1)} %pad.4.k_ref), custom_call_target="tpu_custom_call" | custom-call | tf_op jit(solution)/shard_map/conv_all/pallas_call | solution.py:396
  102.1 1.3 %copy.17 = f32[3,80,480]{1,2,0:T(8,128)S(1)} copy(f32[3,80,480]{2,1,0:T(8,128)} %bitcast.25) | data formatting | bytes 921600 | tf_op jit(solution)/shard_map/slice | solution.py:412
  103.4 0.4 copy.18
  103.8 0.0 copy-start.1
  103.8 1.6 %reshape.38 = f32[9,1,1,12800]{3,2,1,0:T(1,128)} reshape(f32[3,3,80,160]{3,2,1,0:T(8,128)S(1)} %copy.18) | data formatting | bytes 921600 | tf_op jit(solution)/shard_map/reshape | solution.py:416
  105.4 0.0 copy-done.1
  105.4 0.0 copy-start
  105.4 0.8 copy.24
  106.3 0.5 copy-done
  106.8 0.8 copy.25
Async XLA Ops:
  103.8 1.6 %copy-start.1 = (bf16[2,128,1280]{2,1,0:T(8,128)(2,1)S(1)}, bf16[2,128,1280]{2,1,0:T(8,128)(2,1)}, u32[]{:S(2)}) copy-start(bf16[2,128,1280]{2,1,0:T(8,128)(2,1)} %get-tuple-element.6) | copy-start | bytes 1966084
  105.4 1.3 %copy-start = (bf16[16,160,128]{2,1,0:T(8,128)(2,1)S(1)}, bf16[16,160,128]{2,1,0:T(8,128)(2,1)}, u32[]{:S(2)}) copy-start(bf16[16,160,128]{2,1,0:T(8,128)(2,1)} %get-tuple-element.7) | copy-start | bytes 1966084

commit v2 on v1

--- a/solution.py
+++ b/solution.py
@@ -7,7 +7,7 @@
 
 BF = jnp.bfloat16
 F32 = jnp.float32
-N_COPIES = 49
+N_COPIES = 63
 
 
 def dot_nt(a, b):
@@ -24,10 +24,12 @@
 
 
 def body(
-    g_ref, x_ref, k_ref,
-    conv_ref, in_ref, kgrad_ref,
+    g_ref, x_hbm, k_ref,
+    conv_hbm, in_hbm, kgrad_ref,
+    x_ref, conv_ref, in_ref,
     g_pad, gt, kall, xz, xv, xt, f, xa, xb, xl, xr, p, r1, ya, yb, yl, yr, zr,
-    ss, rs, sc,
+    zb, ba, bb, bl, br, lin,
+    ss, rs, sc, lc,
 ):
     t = lax.axis_index("tensor")
     d = lax.axis_index("dp")
@@ -37,6 +39,7 @@
     x_right, x_left, x_far = (x + 1) % 4, (x + 3) % 4, (x + 2) % 4
     y_right, y_left, y_far = (y + 1) % 4, (y + 3) % 4, (y + 2) % 4
     oz = 1 - zh
+    near_half = y // 2
     e_other = y * 2 + 1 - zl
 
     to_z = {"tensor": oz * 4 + x}
@@ -92,16 +95,32 @@
 
     def first_hop(k, which):
         block = 1 - zl if k == 0 else zl
-        return half(r1.at[2 * y_far + block], which), (ya, yb)[which].at[k], (to_yr, to_yl)[which]
+        source = half(r1.at[2 * y_far + block, 0:2], which)
+        return source, (ya, yb)[which].at[k], (to_yr, to_yl)[which]
 
     def second_hop(k, way, which):
         block = 1 - zl if k == 0 else zl
         y_part = (y_right, y_left)[way]
         return (
-            half(r1.at[2 * y_part + block], which),
+            half(r1.at[2 * y_part + block, 0:2], which),
             half((yl, yr)[way].at[k], which),
             (to_yr, to_yl)[way],
         )
+
+    def rows_half(which):
+        return pl.ds(which * 40, 40)
+
+    def z_first(s):
+        return r1.at[2 * part_of(s) + 1 - zl, 2], zb.at[part_of(s)], to_zl
+
+    def tap_first(which):
+        source = r1.at[2 * y_far + zl, 2, rows_half(which)]
+        return source, (ba, bb)[which], (to_yr, to_yl)[which]
+
+    def tap_second(way, which):
+        y_part = (y_right, y_left)[way]
+        source = r1.at[2 * y_part + zl, 2, rows_half(which)]
+        return source, (bl, br)[way].at[rows_half(which)], (to_yr, to_yl)[way]
 
     plan = {
         0: lambda: (g_ref.at[0], row_of(zh, x, 0), to_z),
@@ -109,7 +128,7 @@
         2: lambda: (k_ref, kall.at[e, c, 1], to_z),
         3: lambda: (k_ref, kall.at[e, c, 0], to_zl),
         4: lambda: (k_ref, kall.at[e, c, 1], to_zx),
-        5: lambda: (x_ref.at[pl.ds(7 * oz, 9)], xz, to_z),
+        5: lambda: (x_hbm.at[pl.ds(7 * oz, 9)], xz, to_z),
         6: lambda: (g_ref.at[0], row_of(zh, x, 0), to_xr),
         7: lambda: (g_ref.at[1], row_of(zh, x, 1), to_xr),
         8: lambda: (g_ref.at[1], row_of(zh, x, 1), to_xl),
@@ -120,8 +139,8 @@
         13: lambda: same(row_of(oz, x, 1), to_xr),
         14: lambda: same(row_of(oz, x, 0), to_xl),
         15: lambda: same(row_of(oz, x, 1), to_xl),
-        16: lambda: same(row_of(oz, x_left, 0), to_xr),
-        17: lambda: same(row_of(oz, x_right, 1), to_xl),
+        16: lambda: same(row_of(oz, x_left, 1).at[0:64], to_xr),
+        17: lambda: same(row_of(oz, x_right, 1).at[64:128], to_xl),
         18: lambda: (k_ref, kall.at[e, c, 0], to_yr),
         19: lambda: (k_ref, kall.at[e, c, 0], to_yl),
         20: lambda: same(kall.at[e, c, 1], to_yr),
@@ -134,8 +153,8 @@
         27: lambda: same(pairs(y_left), to_core),
         28: lambda: same(pairs(y_right), to_core),
         29: lambda: same(pairs(y_far), to_core),
-        30: lambda: (f.at[x_far, 0], xa, to_xr),
-        31: lambda: (f.at[x_far, 1], xb, to_xl),
+        30: lambda: (f.at[x_far, 0, near_half], xa.at[near_half], to_xr),
+        31: lambda: (f.at[x_far, 1, near_half], xb.at[near_half], to_xl),
         32: lambda: (f.at[x_right, 1], xl.at[1], to_xr),
         33: lambda: (f.at[x_left, 0], xr.at[0], to_xl),
         34: lambda: (f.at[x_right, 0], xl.at[0], to_xr),
@@ -152,7 +171,20 @@
         45: lambda: second_hop(1, 1, 0),
         46: lambda: second_hop(1, 0, 0),
         47: lambda: second_hop(1, 1, 1),
-        48: lambda: (r1.at[2 * y + 1 - zl], zr, to_zl),
+        48: lambda: (r1.at[2 * y + 1 - zl, 0:2], zr, to_zl),
+        49: lambda: same(row_of(zh, x_far, 0), to_z),
+        50: lambda: (f.at[x_far, 0, 1 - near_half], xa.at[1 - near_half], to_xr),
+        51: lambda: (f.at[x_far, 1, 1 - near_half], xb.at[1 - near_half], to_xl),
+        52: lambda: z_first(0),
+        53: lambda: z_first(1),
+        54: lambda: z_first(2),
+        55: lambda: z_first(3),
+        56: lambda: tap_first(0),
+        57: lambda: tap_first(1),
+        58: lambda: tap_second(0, 1),
+        59: lambda: tap_second(1, 0),
+        60: lambda: tap_second(0, 0),
+        61: lambda: tap_second(1, 1),
     }
 
     def siblings(s):
@@ -165,10 +197,13 @@
             device_id_type=pl.DeviceIdType.MESH,
         )
 
-    start(2, 6, 8, 18, 19, 3, 4, 7, 9, 0, 1, 5)
+    own_g = pltpu.make_async_copy(g_ref, g_pad.at[pl.ds(1 + 2 * t, 2)], lc.at[0])
+    own_x = pltpu.make_async_copy(x_hbm, x_ref, lc.at[1])
+    start(2, 6, 8, 18, 19, 3, 4, 7, 9, 1, 0, 5)
+    own_x.start()
+    own_g.start()
 
     kall[e, c, 0] = k_ref[...]
-    g_pad[pl.ds(1 + 2 * t, 2)] = g_ref[...]
     g_pad[0] = jnp.zeros((128, 1280), BF)
     g_pad[17] = jnp.zeros((128, 1280), BF)
 
@@ -185,6 +220,7 @@
         xv[:, pl.ds(at, 128)] = three_shifts(x_ref[k]).astype(BF)
         return 0
 
+    own_x.wait()
     lax.fori_loop(0, 16, own_row, 0)
 
     got(6)
@@ -205,16 +241,19 @@
     start(20, 21)
     got(3, 4)
     start(22, 23, 26)
+    own_g.wait()
     turn(zh, x)
     got(18, 20)
     start(24)
-    got(0)
-    start(12, 14)
+    got(1)
+    start(13, 15)
     got(7, 9)
     turn(zh, x_left)
     turn(zh, x_right)
-    got(1)
-    start(13, 15)
+    got(10)
+    start(49)
+    got(0)
+    start(12, 14)
     turn(oz, x)
     got(23)
     start(25)
@@ -222,8 +261,10 @@
     start(27)
     got(19, 21)
     start(28)
-    got(12)
+    got(13)
     start(16)
+    got(15)
+    start(17)
     got(5)
 
     def other_turned(k, _):
@@ -232,16 +273,23 @@
 
     lax.fori_loop(0, 9, other_turned, 0)
 
-    got(15)
-    start(17)
-    got(13, 14)
-    turn(oz, x_left)
-    turn(oz, x_right)
-    got(10, 11)
+    got(11)
     turn(zh, x_far)
-    got(24, 25)
-    start(29)
-    got(26, 27, 28, 29)
+
+    def forward_half(xq, h):
+        left = jnp.concatenate(
+            [xt[j, pl.ds(2 * xq + u, 2)].reshape(256, 512) for j in range(2) for u in range(3)],
+            axis=1,
+        )
+        right = jnp.concatenate(
+            [
+                kall[pl.ds(4 * h, 4), :, j, u].reshape(640, 512)
+                for j in range(2)
+                for u in range(3)
+            ],
+            axis=1,
+        )
+        f[xq, :, h] = dot_nt(left, right).reshape(2, 128, 640)
 
     def forward(xq):
         left = jnp.concatenate(
@@ -251,7 +299,9 @@
         right = jnp.concatenate(
             [kall[:, :, j, u].reshape(1280, 512) for j in range(2) for u in range(3)], axis=1
         )
-        f[xq] = dot_nt(left, right).reshape(2, 128, 1280)
+        sums = dot_nt(left, right).reshape(2, 128, 1280)
+        for h in range(2):
+            f[xq, :, h] = sums[:, :, h * 640 : h * 640 + 640]
 
     def kernel_terms(s, _):
         yq = part_of(s)
@@ -272,15 +322,37 @@
         block = 1 - zl if k == 0 else zl
         at = 2 * (y_right, y_left)[way] + block
         rows = slice(way * 40, way * 40 + 40)
-        r1[at, :, rows] = r1[at, :, rows] + (ya, yb)[way][k]
-
-    forward(x_far)
-    start(30, 31)
-    got(16, 17)
+        r1[at, 0:2, rows] = r1[at, 0:2, rows] + (ya, yb)[way][k]
+
+    def add_tap(s):
+        at = 2 * part_of(s) + zl
+        r1[at, 2] = r1[at, 2] + zb[part_of(s)]
+
+    got(26, 27, 28)
+
+    def first_chunk(s, _):
+        h = (near_half + s) % 2
+        forward_half(x_far, h)
+
+        @pl.when(s == 0)
+        def _():
+            start(30, 31)
+            got(24, 25)
+            start(29)
+            got(12, 14)
+            turn(oz, x_left)
+            turn(oz, x_right)
+            got(29)
+
+        return 0
+
+    lax.fori_loop(0, 2, first_chunk, 0)
+    start(50, 51)
+    got(16, 17, 49)
     turn(oz, x_far)
     lax.fori_loop(0, 2, kernel_terms, 0)
     joined(0)
-    start(36, 37, 38, 39)
+    start(36, 37, 38, 39, 52)
 
     def near(s, _):
         forward((x + 1 + 2 * s) % 4)
@@ -293,10 +365,10 @@
 
     lax.fori_loop(0, 2, near, 0)
     start(33)
-    got(30)
+    got(30, 50)
     f[x_right, 0] = f[x_right, 0] + xa[...]
     start(34)
-    got(31)
+    got(31, 51)
     f[x_left, 1] = f[x_left, 1] + xb[...]
     start(35)
 
@@ -306,13 +378,13 @@
         @pl.when(s == 2)
         def _():
             joined(1)
-            start(40)
+            start(40, 53)
 
         return 0
 
     lax.fori_loop(2, 4, last_terms, 0)
     joined(3)
-    start(41)
+    start(41, 55)
     got(36)
     add_half(0, 0)
     start(42)
@@ -326,9 +398,26 @@
     add_half(1, 1)
     start(47)
     joined(2)
+    start(54)
+    got(52)
+    add_tap(0)
+    start(56, 57)
+    got(53)
+    add_tap(1)
+    start(58)
+    got(55)
+    add_tap(3)
+    start(59)
     forward(x)
 
     lane = lax.broadcasted_iota(jnp.int32, (160, 128), 1)
+
+    def put_in(s):
+        rows = pl.ds(4 * s, 4)
+        return pltpu.make_async_copy(in_ref.at[rows], in_hbm.at[rows], lc.at[2 + s])
+
+    def put_conv(k):
+        return pltpu.make_async_copy(conv_ref.at[k], conv_hbm.at[k], lc.at[6 + k])
 
     def input_grad(s, _):
         left = jnp.concatenate(
@@ -341,26 +430,67 @@
             first = jnp.where(lane == 127, 0.0, pltpu.roll(turned[0:160, at], 127, 1))
             last = jnp.where(lane == 0, 0.0, pltpu.roll(turned[320:480, at], 1, 1))
             in_ref[4 * s + k] = (first + turned[160:320, at] + last).astype(BF)
-
-        @pl.when(s == 2)
+        put_in(s).start()
+
+        @pl.when(s == 1)
         def _():
             got(40, 41, 42, 43)
             at = 2 * y + 1 - zl
-            r1[at] = r1[at] + yl[0] + yr[0]
+            r1[at, 0:2] = r1[at, 0:2] + yl[0] + yr[0]
             start(48)
 
+        @pl.when(s == 2)
+        def _():
+            got(56)
+            rows = slice(0, 40)
+            r1[2 * y_right + zl, 2, rows] = r1[2 * y_right + zl, 2, rows] + ba[...]
+            start(60)
+            got(57)
+            rows = slice(40, 80)
+            r1[2 * y_left + zl, 2, rows] = r1[2 * y_left + zl, 2, rows] + bb[...]
+            start(61)
+
         return 0
 
     lax.fori_loop(0, 4, input_grad, 0)
 
+    def spread(u, terms):
+        for q in range(4):
+            lin[q] = terms[:, q * 128 : q * 128 + 128]
+        fours = [
+            jnp.concatenate([lin[q, pl.ds(j, 20, stride=4), :] for q in range(4)], axis=1)
+            for j in range(4)
+        ]
+        for v in range(3):
+            a = [four[:, v * 160 : v * 160 + 160] for four in fours]
+            fives = [
+                a[0][:, :128],
+                jnp.concatenate([a[0][:, 128:], a[1][:, :96]], axis=1),
+                jnp.concatenate([a[1][:, 96:], a[2][:, :64]], axis=1),
+                jnp.concatenate([a[2][:, 64:], a[3][:, :32]], axis=1),
+                a[3][:, 32:],
+            ]
+            for m in range(5):
+                kgrad_ref[pl.ds((3 * u + v) * 100 + m, 20, stride=5), :] = fives[m]
+
+    got(54)
+    add_tap(2)
+    got(44, 45, 46, 47, 48)
+    spread(0, r1[2 * y + zl, 0] + yl[1, 0] + yr[1, 0] + zr[0])
+    spread(1, r1[2 * y + zl, 1] + yl[1, 1] + yr[1, 1] + zr[1])
+    got(58, 59, 60, 61)
+    spread(2, r1[2 * y + zl, 2] + bl[...] + br[...])
     for k, numbers in ((1, (32, 35)), (0, (33, 34))):
         got(*numbers)
-        conv_ref[k] = (f[x, k] + xl[k] + xr[k]).astype(BF)
-    got(44, 45, 46, 47)
-    r1[2 * y + zl] = r1[2 * y + zl] + yl[1] + yr[1]
-    got(48)
-    kgrad_ref[...] = r1[2 * y + zl] + zr[...]
-
+        for h in range(2):
+            total = f[x, k, h] + xl[k, h] + xr[k, h]
+            conv_ref[k, :, h * 640 : h * 640 + 640] = total.astype(BF)
+        put_conv(k).start()
+
+    for s in range(4):
+        put_in(s).wait()
+    for k in range(2):
+        put_conv(k).wait()
     for n in plan:
         copy(n).wait_send()
     for s in range(4):
@@ -373,43 +503,52 @@
     k = kernel.reshape(3, 3, 80, 160).transpose(0, 2, 1, 3).reshape(3, 80, 480)
     k = jnp.pad(k, ((0, 0), (0, 0), (0, 32)))
     vmem = pl.BlockSpec(memory_space=pltpu.VMEM)
+    hbm = pl.BlockSpec(memory_space=pl.ANY)
     scratch = [
+        ((16, 160, 128), BF),
+        ((2, 128, 1280), BF),
+        ((16, 160, 128), BF),
         ((18, 128, 1280), BF),
         ((16, 80, 2048), BF),
         ((8, 2, 2, 3, 80, 512), BF),
         ((9, 160, 128), BF),
         ((512, 2304), BF),
         ((2, 10, 128, 512), BF),
-        ((4, 2, 128, 1280), F32),
-        ((128, 1280), F32),
-        ((128, 1280), F32),
-        ((2, 128, 1280), F32),
-        ((2, 128, 1280), F32),
+        ((4, 2, 2, 128, 640), F32),
+        ((2, 128, 640), F32),
+        ((2, 128, 640), F32),
+        ((2, 2, 128, 640), F32),
+        ((2, 2, 128, 640), F32),
         ((8, 2, 3, 80, 512), F32),
         ((8, 3, 80, 512), F32),
-        ((2, 3, 40, 512), F32),
-        ((2, 3, 40, 512), F32),
-        ((2, 3, 80, 512), F32),
-        ((2, 3, 80, 512), F32),
-        ((3, 80, 512), F32),
+        ((2, 2, 40, 512), F32),
+        ((2, 2, 40, 512), F32),
+        ((2, 2, 80, 512), F32),
+        ((2, 2, 80, 512), F32),
+        ((2, 80, 512), F32),
+        ((4, 80, 512), F32),
+        ((40, 512), F32),
+        ((40, 512), F32),
+        ((80, 512), F32),
+        ((80, 512), F32),
+        ((4, 80, 128), F32),
     ]
     conv, grad, kgrad = pl.pallas_call(
         body,
         out_shape=(
             jax.ShapeDtypeStruct((2, 128, 1280), BF),
             jax.ShapeDtypeStruct((16, 160, 128), BF),
-            jax.ShapeDtypeStruct((3, 80, 512), F32),
+            jax.ShapeDtypeStruct((900, 128), F32),
         ),
-        in_specs=[vmem] * 3,
-        out_specs=(vmem, vmem, vmem),
+        in_specs=[hbm, hbm, vmem],
+        out_specs=(hbm, hbm, vmem),
         scratch_shapes=[pltpu.VMEM(shape, dtype) for shape, dtype in scratch]
-        + [pltpu.SemaphoreType.DMA(shape) for shape in ((N_COPIES,), (N_COPIES,), (2, 4))],
+        + [pltpu.SemaphoreType.DMA(shape) for shape in ((N_COPIES,), (N_COPIES,), (2, 4), (8,))],
         compiler_params=pltpu.CompilerParams(
             collective_id=0, has_side_effects=True, vmem_limit_bytes=67043328
         ),
         name="conv_all",
     )(g, xs, k)
-    kgrad = kgrad[:, :, :480].reshape(3, 80, 3, 160).transpose(0, 2, 1, 3)
     return (
         conv.reshape(2, 1, 128, 1280),
         grad.reshape(16, 1, 160, 128),

time: 108 us -> 102 us (0.944)
  Pallas kernels: 98.8 us -> 93.7 us
    pallas_call x1, Pallas kernels: 98.8 us -> 93.7 us  [on_device(): pl.pallas_call(body, out_shape=(jax.ShapeDtypeStruct((2, 128, 1280), BF),...]
    slice x1 -> x0, local copies, waits for them, and re-layouts: 1.28 us -> none  [on_device(): kgrad = kgrad[:, :, :480].reshape(3, 80, 3, 160).transpose(0, 2, 1, 3)]
where the time goes in v2:
time: 102 us; the launch traced here: 101 us
  Pallas kernels  93.7 us (92%)
  local copies, waits for them, and re-layouts  7.09 us (7%)
    pallas_call x1, Pallas kernels, on_device(): pl.pallas_call(body, out_shape=(jax.ShapeDtypeStruct((2, 128, 1280), BF),...  93.7 us
    reshape x1, local copies, waits for them, and re-layouts, on_device(): kgrad.reshape(9, 1, 1, 12800)  2.3 us
    unnamed x6, local copies, waits for them, and re-layouts  2.16 us

profile of v2, /device:TPU:0, one launch (start us, length us, event | category | flops | bytes accessed | tf_op | source)
XLA Modules:
  0.0 101.5 jit_solution(14952849821784038147)
XLA Ops:
  0.6 1.5 %reshape.29 = bf16[3,3,80,160]{3,2,1,0:T(8,128)(2,1)S(1)} reshape(bf16[9,1,1,12800]{3,0,2,1:T(8,128)(2,1)} %param.4) | data formatting | bytes 460800 | tf_op jit(solution)/shard_map/reshape | solution.py:503
  2.1 0.3 copy.10
  2.4 0.2 copy.11
  2.5 0.7 pad.4.k_ref
  3.3 93.7 %conv_all.1 = (bf16[2,128,1280]{2,1,0:T(8,128)(2,1)}, bf16[16,160,128]{2,1,0:T(8,128)(2,1)}, f32[900,128]{1,0:T(8,128)}) custom-call(bf16[2,128,1280]{2,1,0:T(8,128)(2,1)} %bitcast.14, bf16[16,160,128]{2,1,0:T(8,128)(2,1)} %bitcast.15, bf16[3,80,512]{2,1,0:T(8,128)(2,1)} %pad.4.k_ref), custom_call_target="tpu_custom_call" | custom-call | tf_op jit(solution)/shard_map/conv_all/pallas_call | solution.py:536
  97.0 0.0 copy-start.1
  97.0 2.3 %reshape.34 = f32[9,1,1,12800]{3,2,1,0:T(1,128)} reshape(f32[900,128]{1,0:T(8,128)} %get-tuple-element.8) | data formatting | bytes 921600 | tf_op jit(solution)/shard_map/reshape | solution.py:555
  99.3 0.0 copy-done.1
  99.3 0.0 copy-start
  99.3 0.8 copy.17
  100.2 0.5 copy-done
  100.7 0.8 copy.18
Async XLA Ops:
  97.0 2.3 %copy-start.1 = (bf16[2,128,1280]{2,1,0:T(8,128)(2,1)S(1)}, bf16[2,128,1280]{2,1,0:T(8,128)(2,1)}, u32[]{:S(2)}) copy-start(bf16[2,128,1280]{2,1,0:T(8,128)(2,1)} %get-tuple-element.6) | copy-start | bytes 1966084
  99.3 1.3 %copy-start = (bf16[16,160,128]{2,1,0:T(8,128)(2,1)S(1)}, bf16[16,160,128]{2,1,0:T(8,128)(2,1)}, u32[]{:S(2)}) copy-start(bf16[16,160,128]{2,1,0:T(8,128)(2,1)} %get-tuple-element.7) | copy-start | bytes 1966084
